TPU v7x, 32 devices: a whole 2x2x4 slice. The times are simulated.
32 devices in a mesh: ctx: 8 (over y, x, core), fsdp: 4 (over z).
Axes of the slice: x: 2, y: 2, z: 4, core: 2. Of those that a mesh axis runs over, the one named last changes fastest.
Arguments:
- hidden_in: bfloat16 [4, 1024, 2048], P('fsdp', 'ctx'), may hold values from -18 to 18
- out_grad: bfloat16 [4, 1024, 2048], P('fsdp', 'ctx'), may hold values from -6 to 6
- positions: int32 [4, 1024], P('fsdp', 'ctx'), may hold values from 0 to 1023, as said below
- block_order: int32 [16], replicated, may hold values from 0 to 15, as said below
- attn_gain: float32 [2048], replicated, may hold values from 0.25 to 1.75
- ffn_gain: float32 [2048], replicated, may hold values from 0.25 to 1.75
- qkv_weight: bfloat16 [2048, 3072], P('fsdp'), may hold values from -1 to 1
- out_weight: bfloat16 [2048, 2048], P('fsdp'), may hold values from -0.5 to 0.5
- ffn_weight: bfloat16 [2048, 3, 8192], P(None, None, 'fsdp'), may hold values from -0.125 to 0.125
Outputs:
- hidden_out: bfloat16 [4, 1024, 2048], P('fsdp', 'ctx')
- input_grad: float32 [4, 1024, 2048], P('fsdp', 'ctx')
- qkv_weight_grad: float32 [2048, 3072], P(('ctx', 'fsdp'))
- out_weight_grad: float32 [2048, 2048], P(('ctx', 'fsdp'))
- ffn_weight_grad: float32 [2048, 3, 8192], P('ctx', None, 'fsdp')
- attn_gain_grad: float32 [2048], P(('ctx', 'fsdp'))
- ffn_gain_grad: float32 [2048], P(('ctx', 'fsdp'))
Inputs may be any that keep to these rules, and one draw needn't show every extreme that they name: `block_order`: the two slots 2c and 2c + 1 hold two blocks whose numbers add up to 15, and every block number appears once. In initial token order, a sequence's positions rise by one from token to token and restart at 0 at its first token and at the start of each packed document; the first sequence is a single document; they are listed in storage order.
All inputs are finite; a program needn't handle non-finite values.
Results may differ from a plain program's by a relative error of at most 0.03.
Values may be sent and summed in bfloat16 or wider, within the bound.
No kernel may reach another device: no remote copies, remote signals or barrier semaphores. Data moves between devices by JAX's collectives and lax.ppermute only.
A program may use at most 576 MiB of HBM per device.

v0:
```python
import math
import jax
import jax.numpy as jnp
from jax import lax
from jax.sharding import PartitionSpec as P

H = 32
KV = 8
HD = 64
NORM_EPS = 1e-05
ROPE_BASE = 500000.0
block_rows = 512


def rotate(values, token_places):
    head_dim = values.shape[-1]
    half_dim = head_dim // 2
    frequency = jnp.power(ROPE_BASE, -(jnp.arange(half_dim, dtype=jnp.float32) * 2.0 / head_dim))
    angles = token_places.astype(jnp.float32)[:, None] * frequency[None, :]
    cosine = jnp.concatenate([jnp.cos(angles), jnp.cos(angles)], axis=-1)[:, None, :]
    sine_part = jnp.concatenate([jnp.sin(angles), jnp.sin(angles)], axis=-1)[:, None, :]
    turned = jnp.concatenate([-values[..., half_dim:], values[..., :half_dim]], axis=-1)
    return values * cosine + turned * sine_part


def norm_scale(values):
    return lax.rsqrt(jnp.mean(values * values, axis=-1, keepdims=True) + NORM_EPS)


def lookup(entries, row_ids):
    matches = row_ids[:, None] == jnp.arange(entries.shape[0], dtype=jnp.int32)[None, :]
    return jnp.sum(jnp.where(matches, entries[None, :], 0), axis=1)


def anchor_rows(block_order, first_row, row_count, block_len):
    row_ids = first_row + jnp.arange(row_count, dtype=jnp.int32)
    return lookup(block_order, row_ids // block_len) * block_len + row_ids % block_len


def sweep_keys(step_fn, carried, pieces):
    row_count = pieces[0].shape[0]
    full_blocks = row_count // block_rows

    def loop_step(step_index, carry_state):
        key_pair = tuple(
            (
                lax.dynamic_slice_in_dim(piece_rows, step_index * block_rows, block_rows, 0)
                for piece_rows in pieces
            )
        )
        return step_fn(carry_state, key_pair, step_index * block_rows)

    carried = lax.fori_loop(0, full_blocks, loop_step, carried)
    return carried


def body(
    hidden_in,
    out_grad,
    positions,
    block_order,
    attn_gain,
    ffn_gain,
    qkv_weight,
    out_weight,
    ffn_weight,
):
    local_rows = hidden_in.shape[1]
    block_len = local_rows // 2
    ctx_count = lax.axis_size("ctx")
    seq_rows = local_rows * ctx_count
    groups = H // KV
    score_scale = 1.0 / math.sqrt(HD)
    slot_first = 2 * lax.axis_index("ctx") * block_len
    own_anchor = anchor_rows(block_order, slot_first, local_rows, block_len)
    inputs = hidden_in[0].astype(jnp.float32)
    grad_in = out_grad[0]
    token_places = positions[0]
    scale_one = norm_scale(inputs)
    normed_one = (inputs * scale_one * attn_gain).astype(jnp.bfloat16)
    qkv_full, out_full = (
        lax.all_gather(qkv_weight, "fsdp", axis=0, tiled=True),
        lax.all_gather(out_weight, "fsdp", axis=0, tiled=True),
    )
    projected = jnp.dot(normed_one, qkv_full, preferred_element_type=jnp.float32)
    queries = rotate(projected[:, : H * HD].reshape(local_rows, H, HD), token_places).astype(
        jnp.bfloat16
    )
    queries = queries.reshape(local_rows, KV, groups, HD)
    key_local = rotate(
        projected[:, H * HD : (H + KV) * HD].reshape(local_rows, KV, HD), token_places
    ).astype(jnp.bfloat16)
    key_local = key_local.reshape(local_rows, KV * HD)
    value_local = projected[:, (H + KV) * HD :].astype(jnp.bfloat16)

    def masked_scores(key_heads, first_row, row_count):
        scores = (
            jnp.einsum("tkgd,skd->kgts", queries, key_heads, preferred_element_type=jnp.float32)
            * score_scale
        )
        allowed = (
            anchor_rows(block_order, first_row, row_count, block_len)[None, :]
            <= own_anchor[:, None]
        )[None, None]
        return (jnp.where(allowed, scores, -1e30), allowed)

    def forward_step(carry_state, key_pair, first_row):
        top_old, total_old, summed = carry_state
        key_part, value_part = key_pair
        row_count = key_part.shape[0]
        key_heads = key_part.reshape(row_count, KV, HD)
        value_heads = value_part.reshape(row_count, KV, HD)
        scores, allowed = masked_scores(key_heads, first_row, row_count)
        top_new = jnp.maximum(top_old, jnp.max(scores, axis=-1))
        weights = jnp.where(allowed, jnp.exp(scores - top_new[..., None]), 0.0)
        rescale = jnp.exp(top_old - top_new)
        total_new = total_old * rescale + jnp.sum(weights, axis=-1)
        summed = summed * rescale[..., None] + jnp.einsum(
            "kgts,skd->kgtd",
            weights.astype(jnp.bfloat16),
            value_heads,
            preferred_element_type=jnp.float32,
        )
        return (top_new, total_new, summed)

    start_state = (
        jnp.full((KV, groups, local_rows), -1e30, jnp.float32),
        jnp.zeros((KV, groups, local_rows), jnp.float32),
        jnp.zeros((KV, groups, local_rows, HD), jnp.float32),
    )
    attn_state = sweep_keys(
        forward_step,
        start_state,
        (
            lax.all_gather(key_local, "ctx", axis=0, tiled=True),
            lax.all_gather(value_local, "ctx", axis=0, tiled=True),
        ),
    )
    row_top, row_total, summed = attn_state
    log_total = row_top + jnp.log(row_total)
    attended = (summed / row_total[..., None]).transpose(2, 0, 1, 3)
    attn_rows = attended.reshape(local_rows, H * HD).astype(jnp.bfloat16)
    residual = inputs + jnp.einsum(
        "tc,dc->td", attn_rows, out_full, preferred_element_type=jnp.float32
    )
    scale_two = norm_scale(residual)
    normed_two = (residual * scale_two * ffn_gain).astype(jnp.bfloat16)
    rows_in, rows_out = (
        lax.all_gather(normed_two, "fsdp", axis=0, tiled=True),
        lax.all_gather(grad_in, "fsdp", axis=0, tiled=True),
    )
    weight_piece = lax.all_gather(ffn_weight, "fsdp", axis=2, tiled=True)
    gate_part = jnp.dot(normed_two, weight_piece[:, 0, :], preferred_element_type=jnp.float32)
    up_part = jnp.dot(normed_two, weight_piece[:, 1, :], preferred_element_type=jnp.float32)
    act_part = (gate_part * jax.nn.sigmoid(gate_part) * up_part).astype(jnp.bfloat16)
    out_sum = jnp.einsum(
        "tf,df->td", act_part, weight_piece[:, 2, :], preferred_element_type=jnp.float32
    )
    gate_all = gate_part
    up_all = up_part
    gate_pre = gate_all
    up_pre = up_all
    activated = act_part
    weight_piece = lax.all_gather(ffn_weight, "fsdp", axis=2, tiled=True)
    row_count = weight_piece.shape[2]
    gate_part = gate_pre
    up_part = up_pre
    sig_part = jax.nn.sigmoid(gate_part)
    act_part_grad = jnp.dot(grad_in, weight_piece[:, 2, :], preferred_element_type=jnp.float32)
    gate_part_grad = (
        act_part_grad * up_part * sig_part * (1.0 + gate_part * (1.0 - sig_part))
    ).astype(jnp.bfloat16)
    up_part_grad = (act_part_grad * gate_part * sig_part).astype(jnp.bfloat16)
    sum_grad = jnp.einsum(
        "tf,df->td", gate_part_grad, weight_piece[:, 0, :], preferred_element_type=jnp.float32
    )
    sum_grad = sum_grad + jnp.einsum(
        "tf,df->td", up_part_grad, weight_piece[:, 1, :], preferred_element_type=jnp.float32
    )
    gate_all = gate_part_grad
    up_all = up_part_grad
    gate_grad = gate_all
    up_grad = up_all
    gate_grad, up_grad, activated = (
        lax.all_to_all(gate_grad, "fsdp", split_axis=1, concat_axis=0, tiled=True),
        lax.all_to_all(up_grad, "fsdp", split_axis=1, concat_axis=0, tiled=True),
        lax.all_to_all(activated, "fsdp", split_axis=1, concat_axis=0, tiled=True),
    )
    output = (residual + out_sum).astype(jnp.bfloat16)
    ffn_weight_grad = lax.psum_scatter(
        jnp.stack(
            [
                jnp.einsum("tc,tf->cf", rows_in, gate_grad, preferred_element_type=jnp.float32),
                jnp.einsum("tc,tf->cf", rows_in, up_grad, preferred_element_type=jnp.float32),
                jnp.einsum("tc,tf->cf", rows_out, activated, preferred_element_type=jnp.float32),
            ],
            axis=1,
        ).astype(jnp.bfloat16),
        "ctx",
        scatter_dimension=0,
        tiled=True,
    ).astype(jnp.float32)
    unit_two = residual * scale_two
    ffn_gain_term = jnp.sum(sum_grad * unit_two, axis=0)
    scaled_two = ffn_gain * sum_grad
    residual_grad = grad_in.astype(jnp.float32) + scale_two * (
        scaled_two - unit_two * jnp.mean(scaled_two * unit_two, axis=-1, keepdims=True)
    )
    residual_bf = residual_grad.astype(jnp.bfloat16)
    attn_grad = jnp.dot(residual_bf, out_full, preferred_element_type=jnp.float32).astype(
        jnp.bfloat16
    )
    out_term = jnp.einsum("td,tc->dc", residual_bf, attn_rows, preferred_element_type=jnp.float32)
    attn_grad_heads = attn_grad.reshape(local_rows, KV, groups, HD)
    row_delta = jnp.sum(attn_grad_heads.astype(jnp.float32) * attended, axis=-1).transpose(1, 2, 0)

    def backward_step(carry_state, key_pair, first_row):
        query_grad, key_grad, value_grad = carry_state
        key_part, value_part = key_pair
        row_count = key_part.shape[0]
        key_heads = key_part.reshape(row_count, KV, HD)
        value_heads = value_part.reshape(row_count, KV, HD)
        scores, allowed = masked_scores(key_heads, first_row, row_count)
        probs = jnp.where(allowed, jnp.exp(scores - log_total[..., None]), 0.0)
        value_piece = jnp.einsum(
            "kgts,tkgd->skd",
            probs.astype(jnp.bfloat16),
            attn_grad_heads,
            preferred_element_type=jnp.float32,
        )
        prob_grad = jnp.einsum(
            "tkgd,skd->kgts", attn_grad_heads, value_heads, preferred_element_type=jnp.float32
        )
        score_grad = (probs * (prob_grad - row_delta[..., None]) * score_scale).astype(jnp.bfloat16)
        query_grad = query_grad + jnp.einsum(
            "kgts,skd->tkgd", score_grad, key_heads, preferred_element_type=jnp.float32
        )
        key_piece = jnp.einsum(
            "kgts,tkgd->skd", score_grad, queries, preferred_element_type=jnp.float32
        )
        key_grad = lax.dynamic_update_slice_in_dim(
            key_grad, key_piece.reshape(row_count, KV * HD), first_row, 0
        )
        value_grad = lax.dynamic_update_slice_in_dim(
            value_grad, value_piece.reshape(row_count, KV * HD), first_row, 0
        )
        return (query_grad, key_grad, value_grad)

    start_grads = (
        jnp.zeros((local_rows, KV, groups, HD), jnp.float32),
        jnp.zeros((seq_rows, KV * HD), jnp.float32),
        jnp.zeros((seq_rows, KV * HD), jnp.float32),
    )
    grad_state = sweep_keys(
        backward_step,
        start_grads,
        (
            lax.all_gather(key_local, "ctx", axis=0, tiled=True),
            lax.all_gather(value_local, "ctx", axis=0, tiled=True),
        ),
    )
    query_grad, key_grad_all, value_grad_all = grad_state
    key_grad_own, value_grad_own = (
        lax.psum_scatter(
            key_grad_all.astype(jnp.bfloat16), "ctx", scatter_dimension=0, tiled=True
        ).astype(jnp.float32),
        lax.psum_scatter(
            value_grad_all.astype(jnp.bfloat16), "ctx", scatter_dimension=0, tiled=True
        ).astype(jnp.float32),
    )
    projected_grad = jnp.concatenate(
        [
            rotate(query_grad.reshape(local_rows, H, HD), -token_places).reshape(
                local_rows, H * HD
            ),
            rotate(key_grad_own.reshape(local_rows, KV, HD), -token_places).reshape(
                local_rows, KV * HD
            ),
            value_grad_own,
        ],
        axis=1,
    ).astype(jnp.bfloat16)
    normed_one_grad = jnp.einsum(
        "tc,dc->td", projected_grad, qkv_full, preferred_element_type=jnp.float32
    )
    qkv_term = jnp.einsum(
        "td,tc->dc", normed_one, projected_grad, preferred_element_type=jnp.float32
    )
    unit_one = inputs * scale_one
    attn_gain_term = jnp.sum(normed_one_grad * unit_one, axis=0)
    scaled_one = attn_gain * normed_one_grad
    input_grad = residual_grad + scale_one * (
        scaled_one - unit_one * jnp.mean(scaled_one * unit_one, axis=-1, keepdims=True)
    )
    qkv_grad, out_weight_grad, attn_gain_grad, ffn_gain_grad = (
        lax.psum_scatter(qkv_term, ("ctx", "fsdp"), scatter_dimension=0, tiled=True),
        lax.psum_scatter(out_term, ("ctx", "fsdp"), scatter_dimension=0, tiled=True),
        lax.psum_scatter(attn_gain_term, ("ctx", "fsdp"), scatter_dimension=0, tiled=True),
        lax.psum_scatter(ffn_gain_term, ("ctx", "fsdp"), scatter_dimension=0, tiled=True),
    )
    return (
        output[None],
        input_grad[None],
        qkv_grad,
        out_weight_grad,
        ffn_weight_grad,
        attn_gain_grad,
        ffn_gain_grad,
    )


def solution(mesh):
    return jax.shard_map(
        body,
        mesh=mesh,
        in_specs=(
            P("fsdp", "ctx", None),
            P("fsdp", "ctx", None),
            P("fsdp", "ctx"),
            P(),
            P(),
            P(),
            P("fsdp", None),
            P("fsdp", None),
            P(None, None, "fsdp"),
        ),
        out_specs=(
            P("fsdp", "ctx", None),
            P("fsdp", "ctx", None),
            P(("ctx", "fsdp"), None),
            P(("ctx", "fsdp"), None),
            P("ctx", None, "fsdp"),
            P(("ctx", "fsdp")),
            P(("ctx", "fsdp")),
        ),
        check_vma=False,
    )
```

profile of v0, /device:TPU:0, one launch (start us, length us, event | category | flops | bytes accessed | tf_op | source)
XLA Modules:
  0.0 3142.8 jit_solution(4543832504179743126)
XLA Ops:
  10.9 219.6 %all-gather.9.cloned.1.call-done = bf16[2048,3072]{1,0:T(8,128)(2,1)} async-done(((bf16[512,3072]{1,0:T(8,128)(2,1)}), bf16[2048,3072]{1,0:T(8,128)(2,1)}) %all-gather.9.cloned.1.call-update) | async-done | bytes 12582928 | tf_op jit(solution)/shard_map/all_gather | solution.py:82
  230.5 6.7 fusion.70
  241.2 18.8 all-gather.11.cloned.1.call-done
  261.5 24.4 all-gather.13.cloned.1.call-done
  287.4 33.5 %while.40 = (s32[]{:T(128)}, f32[8,4,128]{2,1,0:T(4,128)S(1)}, f32[8,4,128]{2,1,0:T(4,128)S(1)}, f32[8,4,128,64]{2,3,1,0:T(8,128)}, s32[16]{0:T(128)S(1)}, /*ind...) while((s32[]{:T(128)}, f32[8,4,128]{2,1,0:T(4,128)S(1)}, ...), condition=%wide.region_6.7_spmd.clone, body=%wide.region_2.6_spmd.clone.sunk | while | flops 565045760 | bytes 65024804 | solution.py:53
  293.1 5.8 fusion.136
  323.4 113.5 %all-gather.15.cloned.1.call-done = bf16[2048,2048]{1,0:T(8,128)(2,1)} async-done(((bf16[512,2048]{1,0:T(8,128)(2,1)}), bf16[2048,2048]{1,0:T(8,128)(2,1)}) %all-gather.15.cloned.1.call-update) | async-done | bytes 8388624 | tf_op jit(solution)/shard_map/all_gather | solution.py:83
  436.9 6.5 multiply_reduce_fusion.2
  446.2 1650.2 %all-gather.17.cloned.1.call-done = bf16[2048,3,8192]{2,0,1:T(8,128)(2,1)} async-done(((bf16[2048,3,2048]{2,0,1:T(8,128)(2,1)}), bf16[2048,3,8192]{2,0,1:T(8,128)(2,1)}) %all-gather.17.cloned.1.call-update) | async-done | bytes 100663312 | tf_op jit(solution)/shard_map/all_gather | solution.py:152
  2096.4 15.5 fusion.36
  2112.0 15.2 fusion.38
  2127.1 17.6 multiply_convert_fusion
  2152.3 17.3 fusion.35
  2169.7 20.1 multiply_reduce_fusion
  2204.1 29.0 all-to-all-done.1
  2240.0 40.3 %while.41 = (s32[]{:T(128)}, f32[128,8,4,64]{0,3,2,1:T(8,128)S(1)}, bf16[1024,512]{0,1:T(8,128)(2,1)}, bf16[1024,512]{0,1:T(8,128)(2,1)}, bf16[1024,512]{0,1:T(8...) while((s32[]{:T(128)}, f32[128,8,4,64]{0,3,2,1:T(8,128)S(1)}, ...), condition=%wide.region_12.13_spmd.clone, body=%wide.region_10.12_spmd.clone.sunk | while | flops 1370069504 | bytes 124515376 | solution.py:53
  2242.5 6.0 fusion.151
  2251.7 5.6 fusion.153
  2262.7 6.0 fusion.151
  2292.8 10.4 convert_bitcast_fusion.1
  2303.2 8.5 convert_bitcast_fusion.2
  2311.7 27.3 all-to-all-done.2
  2339.1 10.1 convert_bitcast_fusion
  2349.2 14.2 pad_maximum_fusion
  2364.7 11.5 fusion.66
  2379.9 16.4 fusion.63
  2397.6 17.3 fusion.44
  2414.9 9.4 fusion.56
  2424.3 39.6 %all-reduce.2 = (f32[2048]{0:T(1024)S(1)}, f32[2048]{0:T(1024)S(1)}) all-reduce(f32[2048]{0:T(1024)S(1)} %get-tuple-element.684, f32[2048]{0:T(1024)S(1)} %copy-done.33), channel_id=8, replica_groups=mesh['ctx'=8,'fsdp'=4] {'ctx','fsdp'}, use_global_device_ids=true, to_apply=%region_20.21.clone | all-reduce | flops 4096 | bytes 32768
  2466.4 54.5 %reduce-scatter.14.cloned.1.call-done = bf16[256,3,2048]{2,0,1:T(8,128)(2,1)} async-done(((bf16[2048,3,2048]{2,0,1:T(8,128)(2,1)}), bf16[256,3,2048]{2,0,1:T(8,128)(2,1)}) %reduce-scatter.14.cloned.1.call-update) | async-done | bytes 3145744 | tf_op jit(solution)/shard_map/reduce_scatter | solution.py:190
  2526.3 358.1 %reduce-scatter.12.cloned.1.call-done = f32[64,2048]{1,0:T(8,128)} async-done(((f32[2048,2048]{1,0:T(8,128)}), f32[64,2048]{1,0:T(8,128)}) %reduce-scatter.12.cloned.1.call-update) | async-done | bytes 524304 | tf_op jit(solution)/shard_map/reduce_scatter | solution.py:297
  2884.4 251.3 %reduce-scatter.10.cloned.1.call-done = f32[64,3072]{1,0:T(8,128)} async-done(((f32[2048,3072]{1,0:T(8,128)}), f32[64,3072]{1,0:T(8,128)}) %reduce-scatter.10.cloned.1.call-update) | async-done | bytes 786448 | tf_op jit(solution)/shard_map/reduce_scatter | solution.py:296
  (225 shorter events, 121.2 us)
Async XLA Ops:
  7.2 223.3 %all-gather.9.cloned.1.call-start = ((), (), s32[]{:S(2)}) async-start(), calls=%async_computation.8 | async-start | bytes 15728640 | tf_op jit(solution)/shard_map/all_gather | solution.py:82
  7.9 252.1 %all-gather.11.cloned.1.call-start = ((), (), s32[]{:S(2)}) async-start(), calls=%async_computation.9 | async-start | bytes 1179648 | tf_op jit(solution)/shard_map/all_gather | solution.py:135
  10.9 226.3 %copy-start.31 = (f32[128]{0:T(128)}, f32[128]{0:T(128)S(1)}, u32[]{:S(2)}) copy-start(f32[128]{0:T(128)S(1)} %add_rsqrt_fusion.1) | copy-start | bytes 1540
  238.3 47.6 %all-gather.13.cloned.1.call-start = ((), (), s32[]{:S(2)}) async-start(), calls=%async_computation.10 | async-start | bytes 1179648 | tf_op jit(solution)/shard_map/all_gather | solution.py:136
  239.0 197.9 %all-gather.15.cloned.1.call-start = ((), (), s32[]{:S(2)}) async-start(), calls=%async_computation.11 | async-start | bytes 10485760 | tf_op jit(solution)/shard_map/all_gather | solution.py:83
  239.6 1856.8 %all-gather.17.cloned.1.call-start = ((), (), s32[]{:S(2)}) async-start(), calls=%async_computation.12 | async-start | bytes 125829120 | tf_op jit(solution)/shard_map/all_gather | solution.py:152
  240.2 2052.6 %all-gather.19.cloned.1.call-start = ((), (), s32[]{:S(2)}) async-start(), calls=%async_computation.15 | async-start | bytes 2621440 | tf_op jit(solution)/shard_map/all_gather | solution.py:149
  287.4 149.6 %copy-start.7 = (bf16[1,128,2048]{2,1,0:T(8,128)(2,1)S(1)}, bf16[1,128,2048]{2,1,0:T(8,128)(2,1)}, u32[]{:S(2)}) copy-start(bf16[1,128,2048]{2,1,0:T(8,128)(2,1)} %param.13) | copy-start | bytes 1572868
  293.1 7.6 copy-start
  320.9 125.3 %copy-start.3 = (bf16[1024,512]{0,1:T(8,128)(2,1)}, bf16[1024,512]{0,1:T(8,128)(2,1)S(1)}, u32[]{:S(2)}) copy-start(bf16[1024,512]{0,1:T(8,128)(2,1)S(1)} %get-tuple-element.1013) | copy-start | bytes 3145732
  320.9 123.6 %copy-start.30 = (f32[2048]{0:T(1024)S(1)}, f32[2048]{0:T(1024)}, u32[]{:S(2)}) copy-start(f32[2048]{0:T(1024)} %param.18) | copy-start | bytes 24580
  445.4 1866.3 %all-gather.21.cloned.1.call-start = ((), (), s32[]{:S(2)}) async-start(), calls=%async_computation.17 | async-start | bytes 2621440 | tf_op jit(solution)/shard_map/all_gather | solution.py:150
  446.2 1665.7 %copy-start.24 = (bf16[128,2048]{1,0:T(8,128)(2,1)S(1)}, bf16[128,2048]{1,0:T(8,128)(2,1)}, u32[]{:S(2)}) copy-start(bf16[128,2048]{1,0:T(8,128)(2,1)} %multiply_convert_fusion.3) | copy-start | bytes 1572868
  2147.6 85.5 %all-to-all-start.1 = ((bf16[128,4,2048]{2,0,1:T(8,128)(2,1)}), bf16[128,4,2048]{2,0,1:T(8,128)(2,1)}, u32[]{:S(2)}, u32[]{:S(2)}) async-start(bf16[128,4,2048]{2,0,1:T(8,128)(2,1)} %bitcast.282), calls=%async_computation.3 | async-start | bytes 4194304 | tf_op jit(solution)/shard_map/all_to_all | solution.py:186
  2169.7 20.1 copy-start.25
  2233.1 53.1 %all-to-all-start = ((bf16[128,4,2048]{2,0,1:T(8,128)(2,1)}), bf16[128,4,2048]{2,0,1:T(8,128)(2,1)}, u32[]{:S(2)}, u32[]{:S(2)}) async-start(bf16[128,4,2048]{2,0,1:T(8,128)(2,1)} %bitcast.280), calls=%async_computation.2 | async-start | bytes 4194304 | tf_op jit(solution)/shard_map/all_to_all | solution.py:185
  2237.5 139.9 %reduce-scatter.16.cloned.1.call-start = ((), (), s32[]{:S(2)}) async-start(), calls=%async_computation.18 | async-start | bytes 1179648
  2251.7 8.5 copy-start.22
  2271.8 7.0 copy-start.14
  2271.9 8.5 copy-start.22
  2280.4 10.6 copy-start.18
  2286.2 52.9 %all-to-all-start.2 = ((bf16[128,4,2048]{2,0,1:T(8,128)(2,1)}), bf16[128,4,2048]{2,0,1:T(8,128)(2,1)}, u32[]{:S(2)}, u32[]{:S(2)}) async-start(bf16[128,4,2048]{2,0,1:T(8,128)(2,1)} %bitcast.281), calls=%async_computation.4 | async-start | bytes 4194304 | tf_op jit(solution)/shard_map/all_to_all | solution.py:187
  2290.9 87.9 %reduce-scatter.18.cloned.1.call-start = ((), (), s32[]{:S(2)}) async-start(), calls=%async_computation.19 | async-start | bytes 1179648
  2292.3 228.6 %reduce-scatter.14.cloned.1.call-start = ((), (), s32[]{:S(2)}) async-start(), calls=%async_computation.16 | async-start | bytes 28311552 | tf_op jit(solution)/shard_map/reduce_scatter | solution.py:190
  2292.8 10.4 copy-start.34
  2339.1 10.2 copy-start.11
  2339.1 10.2 copy-start.12
  2363.4 521.0 %reduce-scatter.12.cloned.1.call-start = ((), (), s32[]{:S(2)}) async-start(), calls=%async_computation.14 | async-start | bytes 17301504 | tf_op jit(solution)/shard_map/reduce_scatter | solution.py:297
  2376.3 759.4 %reduce-scatter.10.cloned.1.call-start = ((), (), s32[]{:S(2)}) async-start(), calls=%async_computation.13 | async-start | bytes 25952256 | tf_op jit(solution)/shard_map/reduce_scatter | solution.py:296
  2377.4 18.9 copy-start.19
  2397.6 17.3 copy-start.20
  2414.9 9.4 copy-start.33
  (28 other events, 80.5 us)
Sparse Core Ops, SparseCore 0:
  9.5 220.9 all-gather.8
  238.4 21.5 all-gather.10
  262.5 23.3 all-gather.12
  287.3 149.5 all-gather.14
  438.4 1658.0 all-gather.16
  2098.4 43.8 all-gather.18
  2143.9 83.2 all-gather.20
  2282.9 37.2 reduce-scatter.15
  2323.9 35.9 reduce-scatter.17
  2363.5 157.3 reduce-scatter.13
  2523.8 360.6 reduce-scatter.11
  2891.3 244.3 reduce-scatter.9
where the time goes:
time: 3150 us; the launch traced here: 3140 us
  waiting for transfers between devices  2750 us (87%)
  matrix products  241 us (8%)
  other arithmetic  43.7 us (1%)
  blocking collectives  39.6 us (1%)
  local copies, waits for them, and re-layouts  38.9 us (1%)
    all_gather x1, waiting for transfers between devices, body(): weight_piece = lax.all_gather(ffn_weight, 'fsdp', axis=2, tiled=True)  1650 us
    reduce_scatter x1, waiting for transfers between devices, body(): lax.psum_scatter(out_term, ('ctx', 'fsdp'), scatter_dimension=0, tiled=True)  358 us
    reduce_scatter x1, waiting for transfers between devices, body(): lax.psum_scatter(qkv_term, ('ctx', 'fsdp'), scatter_dimension=0, tiled=True)  251 us
    all_gather x1, waiting for transfers between devices, body(): lax.all_gather(qkv_weight, 'fsdp', axis=0, tiled=True)  220 us
    all_gather x1, waiting for transfers between devices, body(): lax.all_gather(out_weight, 'fsdp', axis=0, tiled=True)  114 us
  transfers between devices with their start and end apart: 15, of which 11 were waited for; matrix products, arithmetic and copies ran while one was open for 10% of the time, Pallas kernels for 0%

commit v1 on v0

--- a/solution.py
+++ b/solution.py
@@ -10,6 +10,11 @@
 NORM_EPS = 1e-05
 ROPE_BASE = 500000.0
 block_rows = 512
+
+
+def exchange_gather(value, axis, dim):
+    outgoing = jnp.stack([value] * lax.axis_size(axis))
+    return jnp.concatenate(lax.all_to_all(outgoing, axis, 0, 0), axis=dim)
 
 
 def rotate(values, token_places):
@@ -79,7 +84,7 @@
     scale_one = norm_scale(inputs)
     normed_one = (inputs * scale_one * attn_gain).astype(jnp.bfloat16)
     qkv_full, out_full = (
-        lax.all_gather(qkv_weight, "fsdp", axis=0, tiled=True),
+        exchange_gather(qkv_weight, "fsdp", 0),
         lax.all_gather(out_weight, "fsdp", axis=0, tiled=True),
     )
     projected = jnp.dot(normed_one, qkv_full, preferred_element_type=jnp.float32)

time: 3150 us -> 3210 us (1.019)
  waiting for transfers between devices: 2750 us -> 2800 us
    all_to_all x0 -> x1, waiting for transfers between devices: none -> 273 us  [exchange_gather(): return jnp.concatenate(lax.all_to_all(outgoing, axis, 0, 0), axis=dim)]
    all_gather x1 -> x0, waiting for transfers between devices: 220 us -> none  [body(): lax.all_gather(qkv_weight, 'fsdp', axis=0, tiled=True)]
  transfers between devices with their start and end apart: 15 -> 15, of which waited for: 11 -> 11; matrix products, arithmetic and copies ran while one was open for 10% -> 9% of each run, Pallas kernels for 0% -> 0%
where the time goes in v1:
time: 3210 us
  waiting for transfers between devices  2800 us (87%)
  matrix products  239 us (7%)
  local copies, waits for them, and re-layouts  44.7 us (1%)
  other arithmetic  42 us (1%)
  blocking collectives  40 us (1%)
    all_gather x1, waiting for transfers between devices, body(): weight_piece = lax.all_gather(ffn_weight, 'fsdp', axis=2, tiled=True)  1650 us
    reduce_scatter x1, waiting for transfers between devices, body(): lax.psum_scatter(out_term, ('ctx', 'fsdp'), scatter_dimension=0, tiled=True)  358 us
    all_to_all x1, waiting for transfers between devices, exchange_gather(): return jnp.concatenate(lax.all_to_all(outgoing, axis, 0, 0), axis=dim)  273 us
    reduce_scatter x1, waiting for transfers between devices, body(): lax.psum_scatter(qkv_term, ('ctx', 'fsdp'), scatter_dimension=0, tiled=True)  251 us
    all_gather x1, waiting for transfers between devices, body(): lax.all_gather(out_weight, 'fsdp', axis=0, tiled=True)  114 us
  transfers between devices with their start and end apart: 15, of which 11 were waited for; matrix products, arithmetic and copies ran while one was open for 9% of the time, Pallas kernels for 0%

profile of v1, /device:TPU:0, one launch (start us, length us, event | category | flops | bytes accessed | tf_op | source)
XLA Modules:
  0.0 3207.7 jit_solution(2866039640158242930)
XLA Ops:
  7.2 8.0 stack.23
  15.2 6.5 all-to-all-start
  22.9 273.4 %all-to-all-done = bf16[4,512,3072]{2,1,0:T(8,128)(2,1)} async-done(((bf16[4,512,3072]{2,1,0:T(8,128)(2,1)}), bf16[4,512,3072]{2,1,0:T(8,128)(2,1)}, u32[]{:S(2)}, u32[]{:S(2)}) %all-to-all-start) | async-done | bytes 12582944 | tf_op jit(solution)/shard_map/all_to_all | solution.py:17
  296.3 6.5 fusion.67
  307.2 19.4 all-gather.8.cloned.1.call-done
  328.1 24.4 all-gather.10.cloned.1.call-done
  354.0 33.5 %while.40 = (s32[]{:T(128)}, f32[8,4,128]{2,1,0:T(4,128)S(1)}, f32[8,4,128]{2,1,0:T(4,128)S(1)}, f32[8,4,128,64]{2,3,1,0:T(8,128)}, s32[16]{0:T(128)S(1)}, /*ind...) while((s32[]{:T(128)}, f32[8,4,128]{2,1,0:T(4,128)S(1)}, ...), condition=%wide.region_6.7_spmd.clone, body=%wide.region_2.6_spmd.clone.sunk | while | flops 565045760 | bytes 65024804 | solution.py:58
  390.0 113.7 %all-gather.12.cloned.1.call-done = bf16[2048,2048]{1,0:T(8,128)(2,1)} async-done(((bf16[512,2048]{1,0:T(8,128)(2,1)}), bf16[2048,2048]{1,0:T(8,128)(2,1)}) %all-gather.12.cloned.1.call-update) | async-done | bytes 8388624 | tf_op jit(solution)/shard_map/all_gather | solution.py:88
  503.7 6.5 multiply_reduce_fusion.2
  512.8 1650.4 %all-gather.14.cloned.1.call-done = bf16[2048,3,8192]{2,0,1:T(8,128)(2,1)} async-done(((bf16[2048,3,2048]{2,0,1:T(8,128)(2,1)}), bf16[2048,3,8192]{2,0,1:T(8,128)(2,1)}) %all-gather.14.cloned.1.call-update) | async-done | bytes 100663312 | tf_op jit(solution)/shard_map/all_gather | solution.py:157
  2163.2 15.5 fusion.36
  2178.7 15.1 fusion.38
  2193.8 17.6 multiply_convert_fusion
  2219.0 17.3 fusion.35
  2236.4 20.1 multiply_reduce_fusion
  2269.8 29.9 all-to-all-done.2
  2306.8 38.7 %while.41 = (s32[]{:T(128)}, f32[128,8,4,64]{0,3,2,1:T(8,128)S(1)}, bf16[1024,512]{0,1:T(8,128)(2,1)}, bf16[1024,512]{0,1:T(8,128)(2,1)}, bf16[1024,512]{0,1:T(8...) while((s32[]{:T(128)}, f32[128,8,4,64]{0,3,2,1:T(8,128)S(1)}, ...), condition=%wide.region_12.13_spmd.clone, body=%wide.region_10.12_spmd.clone.sunk | while | flops 1370069504 | bytes 120321008 | solution.py:58
  2308.5 6.0 fusion.160
  2327.8 6.0 fusion.160
  2358.9 10.4 convert_bitcast_fusion.1
  2369.3 8.4 convert_bitcast_fusion.2
  2377.6 27.4 all-to-all-done.3
  2405.0 10.1 convert_bitcast_fusion
  2415.2 14.2 pad_maximum_fusion
  2430.7 12.1 fusion.78
  2446.3 16.0 fusion.69
  2463.6 17.3 fusion.44
  2480.9 9.4 fusion.58
  2490.3 40.0 %all-reduce.2 = (f32[2048]{0:T(1024)S(1)}, f32[2048]{0:T(1024)S(1)}) all-reduce(f32[2048]{0:T(1024)S(1)} %get-tuple-element.684, f32[2048]{0:T(1024)S(1)} %copy-done.30), channel_id=8, replica_groups=mesh['ctx'=8,'fsdp'=4] {'ctx','fsdp'}, use_global_device_ids=true, to_apply=%region_20.21.clone | all-reduce | flops 4096 | bytes 32768
  2532.7 53.4 %reduce-scatter.14.cloned.1.call-done = bf16[256,3,2048]{2,0,1:T(8,128)(2,1)} async-done(((bf16[2048,3,2048]{2,0,1:T(8,128)(2,1)}), bf16[256,3,2048]{2,0,1:T(8,128)(2,1)}) %reduce-scatter.14.cloned.1.call-update) | async-done | bytes 3145744 | tf_op jit(solution)/shard_map/reduce_scatter | solution.py:195
  2591.6 357.9 %reduce-scatter.12.cloned.1.call-done = f32[64,2048]{1,0:T(8,128)} async-done(((f32[2048,2048]{1,0:T(8,128)}), f32[64,2048]{1,0:T(8,128)}) %reduce-scatter.12.cloned.1.call-update) | async-done | bytes 524304 | tf_op jit(solution)/shard_map/reduce_scatter | solution.py:302
  2949.5 251.4 %reduce-scatter.10.cloned.1.call-done = f32[64,3072]{1,0:T(8,128)} async-done(((f32[2048,3072]{1,0:T(8,128)}), f32[64,3072]{1,0:T(8,128)}) %reduce-scatter.10.cloned.1.call-update) | async-done | bytes 786448 | tf_op jit(solution)/shard_map/reduce_scatter | solution.py:301
  (217 shorter events, 128.5 us)
Async XLA Ops:
  15.2 7.5 copy-start.7
  15.2 281.2 %copy-start.22 = (f32[2048]{0:T(1024)S(1)}, f32[2048]{0:T(1024)}, u32[]{:S(2)}) copy-start(f32[2048]{0:T(1024)} %param.17) | copy-start | bytes 24580
  15.2 281.2 %all-to-all-start = ((bf16[4,512,3072]{2,1,0:T(8,128)(2,1)}), bf16[4,512,3072]{2,1,0:T(8,128)(2,1)}, u32[]{:S(2)}, u32[]{:S(2)}) async-start(bf16[4,512,3072]{2,1,0:T(8,128)(2,1)} %stack.23), calls=%async_computation | async-start | bytes 25165824 | tf_op jit(solution)/shard_map/all_to_all | solution.py:17
  21.7 304.9 %all-gather.8.cloned.1.call-start = ((), (), s32[]{:S(2)}) async-start(), calls=%async_computation.9 | async-start | bytes 1179648 | tf_op jit(solution)/shard_map/all_gather | solution.py:140
  22.9 279.9 %copy-start.28 = (f32[128]{0:T(128)}, f32[128]{0:T(128)S(1)}, u32[]{:S(2)}) copy-start(f32[128]{0:T(128)S(1)} %add_rsqrt_fusion.1) | copy-start | bytes 1540
  303.9 48.5 %all-gather.10.cloned.1.call-start = ((), (), s32[]{:S(2)}) async-start(), calls=%async_computation.10 | async-start | bytes 1179648 | tf_op jit(solution)/shard_map/all_gather | solution.py:141
  304.7 199.0 %all-gather.12.cloned.1.call-start = ((), (), s32[]{:S(2)}) async-start(), calls=%async_computation.11 | async-start | bytes 10485760 | tf_op jit(solution)/shard_map/all_gather | solution.py:88
  305.4 1857.7 %all-gather.14.cloned.1.call-start = ((), (), s32[]{:S(2)}) async-start(), calls=%async_computation.12 | async-start | bytes 125829120 | tf_op jit(solution)/shard_map/all_gather | solution.py:157
  306.0 2052.8 %all-gather.16.cloned.1.call-start = ((), (), s32[]{:S(2)}) async-start(), calls=%async_computation.15 | async-start | bytes 2621440 | tf_op jit(solution)/shard_map/all_gather | solution.py:154
  359.7 7.7 copy-start
  387.4 125.3 %copy-start.3 = (bf16[1024,512]{0,1:T(8,128)(2,1)}, bf16[1024,512]{0,1:T(8,128)(2,1)S(1)}, u32[]{:S(2)}) copy-start(bf16[1024,512]{0,1:T(8,128)(2,1)S(1)} %get-tuple-element.1014) | copy-start | bytes 3145732
  387.4 123.8 %copy-start.27 = (f32[2048]{0:T(1024)S(1)}, f32[2048]{0:T(1024)}, u32[]{:S(2)}) copy-start(f32[2048]{0:T(1024)} %param.18) | copy-start | bytes 24580
  512.2 1865.5 %all-gather.18.cloned.1.call-start = ((), (), s32[]{:S(2)}) async-start(), calls=%async_computation.17 | async-start | bytes 2621440 | tf_op jit(solution)/shard_map/all_gather | solution.py:155
  512.8 1665.9 %copy-start.20 = (bf16[128,2048]{1,0:T(8,128)(2,1)S(1)}, bf16[128,2048]{1,0:T(8,128)(2,1)}, u32[]{:S(2)}) copy-start(bf16[128,2048]{1,0:T(8,128)(2,1)} %multiply_convert_fusion.3) | copy-start | bytes 1572868
  2214.3 85.4 %all-to-all-start.2 = ((bf16[128,4,2048]{2,0,1:T(8,128)(2,1)}), bf16[128,4,2048]{2,0,1:T(8,128)(2,1)}, u32[]{:S(2)}, u32[]{:S(2)}) async-start(bf16[128,4,2048]{2,0,1:T(8,128)(2,1)} %bitcast.309), calls=%async_computation.4 | async-start | bytes 4194304 | tf_op jit(solution)/shard_map/all_to_all | solution.py:191
  2236.4 20.1 copy-start.21
  2299.7 53.1 %all-to-all-start.1 = ((bf16[128,4,2048]{2,0,1:T(8,128)(2,1)}), bf16[128,4,2048]{2,0,1:T(8,128)(2,1)}, u32[]{:S(2)}, u32[]{:S(2)}) async-start(bf16[128,4,2048]{2,0,1:T(8,128)(2,1)} %bitcast.307), calls=%async_computation.3 | async-start | bytes 4194304 | tf_op jit(solution)/shard_map/all_to_all | solution.py:190
  2304.1 139.8 %reduce-scatter.16.cloned.1.call-start = ((), (), s32[]{:S(2)}) async-start(), calls=%async_computation.18 | async-start | bytes 1179648
  2317.7 7.0 copy-start.14
  2317.7 7.0 copy-start.16
  2337.0 7.0 copy-start.14
  2337.0 7.0 copy-start.16
  2345.5 11.8 copy-start.18
  2352.8 52.3 %all-to-all-start.3 = ((bf16[128,4,2048]{2,0,1:T(8,128)(2,1)}), bf16[128,4,2048]{2,0,1:T(8,128)(2,1)}, u32[]{:S(2)}, u32[]{:S(2)}) async-start(bf16[128,4,2048]{2,0,1:T(8,128)(2,1)} %bitcast.308), calls=%async_computation.5 | async-start | bytes 4194304 | tf_op jit(solution)/shard_map/all_to_all | solution.py:192
  2357.2 88.0 %reduce-scatter.18.cloned.1.call-start = ((), (), s32[]{:S(2)}) async-start(), calls=%async_computation.19 | async-start | bytes 1179648
  2358.6 227.6 %reduce-scatter.14.cloned.1.call-start = ((), (), s32[]{:S(2)}) async-start(), calls=%async_computation.16 | async-start | bytes 28311552 | tf_op jit(solution)/shard_map/reduce_scatter | solution.py:195
  2358.9 10.4 copy-start.31
  2405.0 10.1 copy-start.11
  2405.0 10.1 copy-start.12
  2429.4 520.2 %reduce-scatter.12.cloned.1.call-start = ((), (), s32[]{:S(2)}) async-start(), calls=%async_computation.14 | async-start | bytes 17301504 | tf_op jit(solution)/shard_map/reduce_scatter | solution.py:302
  2442.8 758.1 %reduce-scatter.10.cloned.1.call-start = ((), (), s32[]{:S(2)}) async-start(), calls=%async_computation.13 | async-start | bytes 25952256 | tf_op jit(solution)/shard_map/reduce_scatter | solution.py:301
  2480.9 9.4 copy-start.30
  (24 other events, 64.0 us)
Sparse Core Ops, SparseCore 0:
  304.1 22.4 all-gather.7
  329.1 23.3 all-gather.9
  354.0 149.5 all-gather.11
  505.1 1658.0 all-gather.13
  2165.2 43.8 all-gather.15
  2210.5 83.1 all-gather.17
  2348.0 37.2 reduce-scatter.15
  2389.1 35.9 reduce-scatter.17
  2429.5 156.6 reduce-scatter.13
  2588.9 360.5 reduce-scatter.11
  2956.5 244.3 reduce-scatter.9
